TPU v7x, 256 devices: a whole 4x4x8 slice. The times are simulated.
256 devices in a mesh: dst: 32 (over y, z), src: 8 (over x, core).
Axes of the slice: x: 4, y: 4, z: 8, core: 2. Of those that a mesh axis runs over, the one named last changes fastest.
Arguments:
- transitions: bfloat16 [16384, 128, 128], P(('dst', 'src')), may hold values from 0.0009994507 to 1
- row_block: int32 [16384], P(('dst', 'src')), may hold values from -1 to 1023, as said below
- col_block: int32 [16384], P(('dst', 'src')), may hold values from -1 to 1023, as said below
- beta_last: float32 [32, 128, 8, 128], P(None, 'dst', 'src'), may hold values from 0.2 to 2
- emissions: bfloat16 [2, 32, 128, 8, 128], P(None, None, 'dst', 'src'), may hold values from 0.019897461 to 1
- forward: bfloat16 [2, 32, 128, 8, 128], P(None, None, 'dst', 'src'), may hold values from 0.03 to 125, as said below
Outputs:
- counts: bfloat16 [16384, 128, 128], P(('dst', 'src'))
- beta_first: float32 [32, 128, 8, 128], P(None, 'dst', 'src')
- log_norms: float32 [2, 32], replicated
Inputs may be any that keep to these rules, and one draw needn't show every extreme that they name: `row_block`: slots are grouped by device (index dst * 8 + src), 64 to a device. A live slot holds a block whose source block number r has r % 8 equal to the device's src index and whose destination block lies in the device's dst index's own consecutive equal share of blocks; no block appears twice; live slots come first, and empty ones hold -1 in both arrays. One device has all 64 slots live; each device has at least one. `col_block`: same slots as row_block; -1 exactly where row_block is -1. `forward`: Positive.
All inputs are finite; a program needn't handle non-finite values.
Results may differ from a plain program's by a relative error of at most 0.0029.
Values may be sent and summed in bfloat16 or wider, within the bound.
No kernel may reach another device: no remote copies, remote signals or barrier semaphores. Data moves between devices by JAX's collectives and lax.ppermute only.
A program may use at most 64 MiB of HBM per device.

v0:
```python
import jax
import jax.numpy as jnp
from jax import lax
from jax.sharding import PartitionSpec as P

S = 131072
STEPS = 2


def body(transitions, row_block, col_block, beta_last, emissions, forward):
    source_count = lax.axis_size("src")
    seq_count = beta_last.shape[0]
    local_rows = beta_last.shape[1]
    block_size = beta_last.shape[3]
    slot_count = transitions.shape[0]
    column_count = local_rows * source_count
    total_rows = local_rows * lax.axis_size("dst")
    living = row_block >= 0
    live_float = living.astype(jnp.float32)
    row_local = jnp.where(living, row_block // source_count, 0)
    col_local = jnp.where(living, col_block % column_count, 0)
    beta_piece = beta_last[:, :, 0, :]
    count_sum = jnp.zeros((slot_count, block_size, block_size), jnp.float32)
    log_list = []
    for step_index in range(STEPS):
        emitted = emissions[step_index][:, :, 0, :]
        message = (emitted.astype(jnp.float32) * beta_piece).astype(jnp.bfloat16)
        columns = lax.all_gather(message[:, :, None, :], "src", axis=2, tiled=True)
        columns = columns.reshape(seq_count, column_count, block_size)
        alpha_rows = lax.all_gather(forward[step_index], "dst", axis=1, tiled=True)
        alpha_rows = alpha_rows.reshape(seq_count, total_rows, block_size)
        alpha_picked = jnp.take(alpha_rows, row_local, axis=1)
        picked = jnp.take(columns, col_local, axis=1)
        products = jnp.einsum(
            "bcj,cij->cbi", picked, transitions, preferred_element_type=jnp.float32
        )
        products = products * live_float[:, None, None]
        partial_value = jax.ops.segment_sum(products, row_local, num_segments=total_rows)
        raw_sums = lax.psum_scatter(partial_value, "dst", scatter_dimension=0, tiled=True)
        own_alpha = forward[step_index][:, :, 0, :]
        local_term = jnp.einsum(
            "kbr,bkr->b", raw_sums, own_alpha, preferred_element_type=jnp.float32
        )
        scale_now = lax.psum(local_term, ("dst", "src")) / S
        beta_piece = jnp.transpose(raw_sums / scale_now[None, :, None], (1, 0, 2))
        scaled = (columns.astype(jnp.float32) / scale_now[:, None, None]).astype(jnp.bfloat16)
        scaled_picked = jnp.take(scaled, col_local, axis=1)
        count_sum = count_sum + jnp.einsum(
            "bci,bcj->cij", alpha_picked, scaled_picked, preferred_element_type=jnp.float32
        )
        log_list.append(jnp.log(scale_now))
    counts = (count_sum * transitions.astype(jnp.float32) * live_float[:, None, None]).astype(
        jnp.bfloat16
    )
    return (counts, beta_piece[:, :, None, :], jnp.stack(log_list))


def solution(mesh):
    return jax.shard_map(
        body,
        mesh=mesh,
        in_specs=(
            P(("dst", "src"), None, None),
            P(("dst", "src")),
            P(("dst", "src")),
            P(None, "dst", "src", None),
            P(None, None, "dst", "src", None),
            P(None, None, "dst", "src", None),
        ),
        out_specs=(P(("dst", "src"), None, None), P(None, "dst", "src", None), P()),
        check_vma=False,
    )
```

profile of v0, /device:TPU:1, one launch (start us, length us, event | category | flops | bytes accessed | tf_op | source)
XLA Modules:
  0.0 728.8 jit_solution(5440016924613923832)
XLA Ops:
  7.2 0.0 copy-start
  7.2 0.0 reduce-scatter.3.cloned.1.call-start
  7.2 0.8 compare_and_fusion
  8.1 0.0 copy-start.5
  8.1 0.8 fusion.35
  8.9 0.9 fusion.24
  9.7 15.9 %all_gather.13 = bf16[32,4,8,128]{3,0,1,2:T(8,128)(2,1)S(1)} all-gather(bf16[32,4,1,128]{3,0,1,2:T(8,128)(2,1)S(1)} %fusion.24), channel_id=1, replica_groups=mesh['dst'=32,'src'=8] {'src'}, dimensions={2}, use_global_device_ids=true | all-gather | bytes 294912 | tf_op jit(solution)/shard_map/all_gather | solution.py:28
  25.6 0.2 copy.68
  25.8 0.1 copy.34
  25.9 1.4 gather_fusion.1
  27.3 0.0 copy-done
  27.3 2.3 convolution_multiply_fusion.1
  29.6 1.6 broadcast.28.clone
  31.2 0.0 copy-done.5
  31.2 0.0 copy-start.4
  31.2 8.0 %scatter_fusion = f32[128,32,128]{2,1,0:T(8,128)} fusion(f32[128,32,128]{2,1,0:T(8,128)} %broadcast.28.clone, s32[64]{0:T(128)S(1)} %get-tuple-element.28, f32[64,32,128]{2,1,0:T(8,128)S(1)} %convolution_multiply_fusion.1), kind=kCustom, calls=%fused_computation.6 | custom fusion | flops 262144 | bytes 3145984 | tf_op jit(solution)/shard_map/scatter-add | solution.py:38
  39.2 0.0 reduce-scatter.3.cloned.1.call-update
  39.3 0.0 all-gather.8.cloned.1.call-start
  39.3 0.0 copy-done.4
  39.4 0.6 copy.54
  40.0 0.0 all-gather.8.cloned.1.call-update
  40.0 0.0 all-gather.6.cloned.1.call-start
  40.1 0.6 copy.52
  40.7 0.1 all-gather.6.cloned.1.call-update
  40.8 0.0 reduce-scatter.5.cloned.1.call-start
  40.8 213.9 %reduce-scatter.3.cloned.1.call-done = f32[4,32,128]{2,1,0:T(8,128)} async-done(((f32[128,32,128]{2,1,0:T(8,128)}), f32[4,32,128]{2,1,0:T(8,128)}) %reduce-scatter.3.cloned.1.call-update) | async-done | bytes 65552 | tf_op jit(solution)/shard_map/reduce_scatter | solution.py:39
  254.7 1.0 multiply_reduce_fusion.1
  255.7 79.9 %psum.14 = f32[32]{0:T(128)S(1)} all-reduce(f32[32]{0:T(128)S(1)} %multiply_reduce_fusion.1), channel_id=1, replica_groups=mesh['dst'=32,'src'=8] {'dst','src'}, use_global_device_ids=true, to_apply=%region_2.5 | all-reduce | flops 32 | bytes 256 | tf_op jit(solution)/shard_map/psum | solution.py:44
  335.6 0.9 fusion.23
  336.5 12.6 %all-gather.2 = bf16[32,4,1024]{2,0,1:T(8,128)(2,1)S(1)} all-gather(bf16[32,4,128]{2,0,1:T(8,128)(2,1)S(1)} %fusion.23), channel_id=4, replica_groups=mesh['dst'=32,'src'=8] {'src'}, dimensions={2}, use_global_device_ids=true | all-gather | bytes 294912 | tf_op jit(solution)/shard_map/all_gather | solution.py:28
  349.1 0.2 copy.38
  349.3 0.1 reshape.50
  349.4 0.0 copy-start.1
  349.4 0.1 copy.39
  349.5 0.6 copy-done.1
  350.1 1.4 gather_fusion.4
  351.6 0.0 copy-start.6
  351.6 2.3 convolution_multiply_fusion
  353.8 1.6 broadcast.28
  355.4 0.0 copy-done.6
  355.4 8.0 %scatter_fusion.1 = f32[128,32,128]{2,1,0:T(8,128)} fusion(f32[128,32,128]{2,1,0:T(8,128)} %broadcast.28, s32[64]{0:T(128)S(1)} %copy-done.6, f32[64,32,128]{2,1,0:T(8,128)S(1)} %convolution_multiply_fusion), kind=kCustom, calls=%fused_computation.7 | custom fusion | flops 262144 | bytes 3145984 | tf_op jit(solution)/shard_map/scatter-add | solution.py:38
  363.5 0.0 reduce-scatter.5.cloned.1.call-update
  363.5 0.0 all-gather.8.cloned.1.call-done
  363.6 1.9 gather_fusion.3
  365.5 43.8 %all-gather.6.cloned.1.call-done = bf16[1,32,128,1,128]{4,1,3,0,2:T(8,128)(2,1)} async-done(((bf16[1,32,4,1,128]{4,1,3,0,2:T(8,128)(2,1)}), bf16[1,32,128,1,128]{4,1,3,0,2:T(8,128)(2,1)}) %all-gather.6.cloned.1.call-update) | async-done | bytes 1048592 | tf_op jit(solution)/shard_map/all_gather | solution.py:30
  409.3 2.6 gather_fusion
  411.9 0.1 divide_convert_fusion.1
  412.0 1.4 gather_fusion.2
  413.5 216.1 %reduce-scatter.5.cloned.1.call-done = f32[4,32,128]{2,1,0:T(8,128)} async-done(((f32[128,32,128]{2,1,0:T(8,128)}), f32[4,32,128]{2,1,0:T(8,128)}) %reduce-scatter.5.cloned.1.call-update) | async-done | bytes 65552 | tf_op jit(solution)/shard_map/reduce_scatter | solution.py:39
  629.6 1.0 multiply_reduce_fusion
  630.6 0.0 copy-start.2
  630.6 0.0 copy-start.3
  630.6 4.1 fusion.3
  634.7 79.6 %psum.15 = f32[32]{0:T(128)S(1)} all-reduce(f32[32]{0:T(128)S(1)} %multiply_reduce_fusion), channel_id=1, replica_groups=mesh['dst'=32,'src'=8] {'dst','src'}, use_global_device_ids=true, to_apply=%region_5.8 | all-reduce | flops 32 | bytes 256 | tf_op jit(solution)/shard_map/psum | solution.py:44
  714.3 0.0 copy-done.2
  714.3 0.1 divide_convert_fusion
  714.4 0.0 copy-done.3
  714.5 0.1 divide_bitcast_fusion
  714.5 0.7 copy.41
  715.2 1.4 gather_fusion.5
  716.6 0.6 pad_maximum_fusion
  717.2 5.0 multiply_convert_fusion
  (6 shorter events, 0.1 us)
Async XLA Ops:
  7.2 20.2 %copy-start = (bf16[64,128,128]{2,1,0:T(8,128)(2,1)S(1)}, bf16[64,128,128]{2,1,0:T(8,128)(2,1)}, u32[]{:S(2)}) copy-start(bf16[64,128,128]{2,1,0:T(8,128)(2,1)} %param.10) | copy-start | bytes 6291460
  7.2 247.6 %reduce-scatter.3.cloned.1.call-start = ((), (), s32[]{:S(2)}) async-start(), calls=%async_computation.2 | async-start | bytes 2162688 | tf_op jit(solution)/shard_map/reduce_scatter | solution.py:39
  8.1 23.1 %copy-start.5 = (s32[64]{0:T(128)}, s32[64]{0:T(128)S(1)}, u32[]{:S(2)}) copy-start(s32[64]{0:T(128)S(1)} %get-tuple-element.28) | copy-start | bytes 772
  31.2 8.1 %copy-start.4 = (bf16[2,32,4,1,128]{4,2,3,1,0:T(4,128)(2,1)S(1)}, bf16[2,32,4,1,128]{4,2,3,1,0:T(4,128)(2,1)}, u32[]{:S(2)}) copy-start(bf16[2,32,4,1,128]{4,2,3,1,0:T(4,128)(2,1)} %param.15) | copy-start | bytes 196612
  39.3 324.3 %all-gather.8.cloned.1.call-start = ((), (), s32[]{:S(2)}) async-start(), calls=%async_computation.5 | async-start | bytes 1081344 | tf_op jit(solution)/shard_map/all_gather | solution.py:30
  40.0 369.3 %all-gather.6.cloned.1.call-start = ((), (), s32[]{:S(2)}) async-start(), calls=%async_computation.4 | async-start | bytes 1081344 | tf_op jit(solution)/shard_map/all_gather | solution.py:30
  40.8 588.9 %reduce-scatter.5.cloned.1.call-start = ((), (), s32[]{:S(2)}) async-start(), calls=%async_computation.3 | async-start | bytes 2162688 | tf_op jit(solution)/shard_map/reduce_scatter | solution.py:39
  349.4 0.7 copy-start.1
  351.6 3.9 copy-start.6
  630.6 83.8 %copy-start.2 = (bf16[32,32,128]{2,1,0:T(8,128)(2,1)S(1)}, bf16[32,32,128]{2,1,0:T(8,128)(2,1)}, u32[]{:S(2)}) copy-start(bf16[32,32,128]{2,1,0:T(8,128)(2,1)} %copy-done.1) | copy-start | bytes 786436
  630.6 83.9 %copy-start.3 = (f32[4,32,128]{2,1,0:T(8,128)S(1)}, f32[4,32,128]{2,1,0:T(8,128)}, u32[]{:S(2)}) copy-start(f32[4,32,128]{2,1,0:T(8,128)} %reduce-scatter.5.cloned.1.call-done) | copy-start | bytes 196612
Sparse Core Ops, SparseCore 0:
  39.4 215.2 reduce-scatter.2
  257.3 74.8 all-gather.7
  335.4 73.8 all-gather.5
  413.5 216.0 reduce-scatter.4
where the time goes:
time: 730 us; the launch traced here: 729 us
  waiting for transfers between devices  474 us (65%)
  blocking collectives  188 us (26%)
  other arithmetic  21.5 us (3%)
  local copies, waits for them, and re-layouts  17.5 us (2%)
  between operations  13.9 us (2%)
  matrix products  13.7 us (2%)
    reduce_scatter x2, waiting for transfers between devices, body(): lax.psum_scatter(partial_value, 'dst', scatter_dimension=0, tiled=True)  430 us
    psum x2, blocking collectives, body(): scale_now = lax.psum(local_term, ('dst', 'src')) / S  160 us
    all_gather x2, waiting for transfers between devices, body(): alpha_rows = lax.all_gather(forward[step_index], 'dst', axis=1, tiled=True)  43.8 us
    all_gather x2, blocking collectives, body(): columns = lax.all_gather(message[:, :, None, :], 'src', axis=2, tiled=True)  28.5 us
    scatter-add x2, other arithmetic, body(): jax.ops.segment_sum(products, row_local, num_segments=total_rows)  16.1 us
  transfers between devices with their start and end apart: 4, of which 3 were waited for; matrix products, arithmetic and copies ran while one was open for 3% of the time, Pallas kernels for 0%

commit v1 on v0

--- a/solution.py
+++ b/solution.py
@@ -27,7 +27,9 @@
         message = (emitted.astype(jnp.float32) * beta_piece).astype(jnp.bfloat16)
         columns = lax.all_gather(message[:, :, None, :], "src", axis=2, tiled=True)
         columns = columns.reshape(seq_count, column_count, block_size)
-        alpha_rows = lax.all_gather(forward[step_index], "dst", axis=1, tiled=True)
+        view = forward[step_index]
+        z2 = jax.lax.all_gather(view, axis_name="dst")
+        alpha_rows = jnp.concatenate(z2, axis=1)
         alpha_rows = alpha_rows.reshape(seq_count, total_rows, block_size)
         alpha_picked = jnp.take(alpha_rows, row_local, axis=1)
         picked = jnp.take(columns, col_local, axis=1)

time: 730 us -> 730 us (level)
  no operation moved by 1% of the time
where the time goes in v1:
time: 730 us; the launch traced here: 729 us
  waiting for transfers between devices  474 us (65%)
  blocking collectives  188 us (26%)
  other arithmetic  21.5 us (3%)
  local copies, waits for them, and re-layouts  17.5 us (2%)
  between operations  13.9 us (2%)
  matrix products  13.7 us (2%)
    reduce_scatter x2, waiting for transfers between devices, body(): lax.psum_scatter(partial_value, 'dst', scatter_dimension=0, tiled=True)  430 us
    psum x2, blocking collectives, body(): scale_now = lax.psum(local_term, ('dst', 'src')) / S  160 us
    all_gather x2, waiting for transfers between devices, body(): z2 = jax.lax.all_gather(view, axis_name='dst')  43.8 us
    all_gather x2, blocking collectives, body(): columns = lax.all_gather(message[:, :, None, :], 'src', axis=2, tiled=True)  28.5 us
    scatter-add x2, other arithmetic, body(): jax.ops.segment_sum(products, row_local, num_segments=total_rows)  16.1 us
  transfers between devices with their start and end apart: 4, of which 3 were waited for; matrix products, arithmetic and copies ran while one was open for 3% of the time, Pallas kernels for 0%

profile of v1, /device:TPU:1, one launch (start us, length us, event | category | flops | bytes accessed | tf_op | source)
XLA Modules:
  0.0 728.8 jit_solution(5440016924613923832)
XLA Ops:
  7.2 0.0 copy-start
  7.2 0.0 reduce-scatter.3.cloned.1.call-start
  7.2 0.8 compare_and_fusion
  8.1 0.0 copy-start.5
  8.1 0.8 fusion.35
  8.9 0.9 fusion.24
  9.7 15.9 %all_gather.13 = bf16[32,4,8,128]{3,0,1,2:T(8,128)(2,1)S(1)} all-gather(bf16[32,4,1,128]{3,0,1,2:T(8,128)(2,1)S(1)} %fusion.24), channel_id=1, replica_groups=mesh['dst'=32,'src'=8] {'src'}, dimensions={2}, use_global_device_ids=true | all-gather | bytes 294912 | tf_op jit(solution)/shard_map/all_gather | solution.py:28
  25.6 0.2 copy.68
  25.8 0.1 copy.33
  25.9 1.4 gather_fusion.1
  27.3 0.0 copy-done
  27.3 2.3 convolution_multiply_fusion.1
  29.6 1.6 broadcast.28.clone
  31.2 0.0 copy-done.5
  31.2 0.0 copy-start.4
  31.2 8.0 %scatter_fusion = f32[128,32,128]{2,1,0:T(8,128)} fusion(f32[128,32,128]{2,1,0:T(8,128)} %broadcast.28.clone, s32[64]{0:T(128)S(1)} %get-tuple-element.28, f32[64,32,128]{2,1,0:T(8,128)S(1)} %convolution_multiply_fusion.1), kind=kCustom, calls=%fused_computation.6 | custom fusion | flops 262144 | bytes 3145984 | tf_op jit(solution)/shard_map/scatter-add | solution.py:40
  39.2 0.0 reduce-scatter.3.cloned.1.call-update
  39.3 0.0 all-gather.6.cloned.1.call-start
  39.3 0.0 copy-done.4
  39.4 0.6 copy.54
  40.0 0.0 all-gather.6.cloned.1.call-update
  40.0 0.0 all-gather.4.cloned.1.call-start
  40.1 0.6 copy.52
  40.7 0.1 all-gather.4.cloned.1.call-update
  40.8 0.0 reduce-scatter.5.cloned.1.call-start
  40.8 213.9 %reduce-scatter.3.cloned.1.call-done = f32[4,32,128]{2,1,0:T(8,128)} async-done(((f32[128,32,128]{2,1,0:T(8,128)}), f32[4,32,128]{2,1,0:T(8,128)}) %reduce-scatter.3.cloned.1.call-update) | async-done | bytes 65552 | tf_op jit(solution)/shard_map/reduce_scatter | solution.py:41
  254.7 1.0 multiply_reduce_fusion.1
  255.7 79.9 %psum.14 = f32[32]{0:T(128)S(1)} all-reduce(f32[32]{0:T(128)S(1)} %multiply_reduce_fusion.1), channel_id=1, replica_groups=mesh['dst'=32,'src'=8] {'dst','src'}, use_global_device_ids=true, to_apply=%region_2.5 | all-reduce | flops 32 | bytes 256 | tf_op jit(solution)/shard_map/psum | solution.py:46
  335.6 0.9 fusion.23
  336.5 12.6 %all-gather = bf16[32,4,1024]{2,0,1:T(8,128)(2,1)S(1)} all-gather(bf16[32,4,128]{2,0,1:T(8,128)(2,1)S(1)} %fusion.23), channel_id=2, replica_groups=mesh['dst'=32,'src'=8] {'src'}, dimensions={2}, use_global_device_ids=true | all-gather | bytes 294912 | tf_op jit(solution)/shard_map/all_gather | solution.py:28
  349.1 0.2 copy.38
  349.3 0.1 reshape.50
  349.4 0.0 copy-start.1
  349.4 0.1 copy.39
  349.5 0.6 copy-done.1
  350.1 1.4 gather_fusion.4
  351.6 0.0 copy-start.6
  351.6 2.3 convolution_multiply_fusion
  353.8 1.6 broadcast.28
  355.4 0.0 copy-done.6
  355.4 8.0 %scatter_fusion.1 = f32[128,32,128]{2,1,0:T(8,128)} fusion(f32[128,32,128]{2,1,0:T(8,128)} %broadcast.28, s32[64]{0:T(128)S(1)} %copy-done.6, f32[64,32,128]{2,1,0:T(8,128)S(1)} %convolution_multiply_fusion), kind=kCustom, calls=%fused_computation.7 | custom fusion | flops 262144 | bytes 3145984 | tf_op jit(solution)/shard_map/scatter-add | solution.py:40
  363.5 0.0 reduce-scatter.5.cloned.1.call-update
  363.5 0.0 all-gather.6.cloned.1.call-done
  363.6 1.9 gather_fusion.3
  365.5 43.8 %all-gather.4.cloned.1.call-done = bf16[32,32,4,1,128]{4,1,3,2,0:T(8,128)(2,1)} async-done(((bf16[1,32,4,1,128]{4,1,3,2,0:T(8,128)(2,1)}), bf16[32,32,4,1,128]{4,1,3,2,0:T(8,128)(2,1)}) %all-gather.4.cloned.1.call-update) | async-done | bytes 1048592 | tf_op jit(solution)/shard_map/all_gather | solution.py:31
  409.3 2.6 gather_fusion
  411.9 0.1 divide_convert_fusion.1
  412.0 1.4 gather_fusion.2
  413.5 216.1 %reduce-scatter.5.cloned.1.call-done = f32[4,32,128]{2,1,0:T(8,128)} async-done(((f32[128,32,128]{2,1,0:T(8,128)}), f32[4,32,128]{2,1,0:T(8,128)}) %reduce-scatter.5.cloned.1.call-update) | async-done | bytes 65552 | tf_op jit(solution)/shard_map/reduce_scatter | solution.py:41
  629.6 1.0 multiply_reduce_fusion
  630.6 0.0 copy-start.2
  630.6 0.0 copy-start.3
  630.6 4.1 fusion.3
  634.7 79.6 %psum.15 = f32[32]{0:T(128)S(1)} all-reduce(f32[32]{0:T(128)S(1)} %multiply_reduce_fusion), channel_id=1, replica_groups=mesh['dst'=32,'src'=8] {'dst','src'}, use_global_device_ids=true, to_apply=%region_5.8 | all-reduce | flops 32 | bytes 256 | tf_op jit(solution)/shard_map/psum | solution.py:46
  714.3 0.0 copy-done.2
  714.3 0.1 divide_convert_fusion
  714.4 0.0 copy-done.3
  714.5 0.1 divide_bitcast_fusion
  714.5 0.7 copy.41
  715.2 1.4 gather_fusion.5
  716.6 0.6 pad_maximum_fusion
  717.2 5.0 multiply_convert_fusion
  (6 shorter events, 0.1 us)
Async XLA Ops:
  7.2 20.2 %copy-start = (bf16[64,128,128]{2,1,0:T(8,128)(2,1)S(1)}, bf16[64,128,128]{2,1,0:T(8,128)(2,1)}, u32[]{:S(2)}) copy-start(bf16[64,128,128]{2,1,0:T(8,128)(2,1)} %param.10) | copy-start | bytes 6291460
  7.2 247.6 %reduce-scatter.3.cloned.1.call-start = ((), (), s32[]{:S(2)}) async-start(), calls=%async_computation.3 | async-start | bytes 2162688 | tf_op jit(solution)/shard_map/reduce_scatter | solution.py:41
  8.1 23.1 %copy-start.5 = (s32[64]{0:T(128)}, s32[64]{0:T(128)S(1)}, u32[]{:S(2)}) copy-start(s32[64]{0:T(128)S(1)} %get-tuple-element.28) | copy-start | bytes 772
  31.2 8.1 %copy-start.4 = (bf16[2,32,4,1,128]{4,2,3,1,0:T(4,128)(2,1)S(1)}, bf16[2,32,4,1,128]{4,2,3,1,0:T(4,128)(2,1)}, u32[]{:S(2)}) copy-start(bf16[2,32,4,1,128]{4,2,3,1,0:T(4,128)(2,1)} %param.15) | copy-start | bytes 196612
  39.3 324.3 %all-gather.6.cloned.1.call-start = ((), (), s32[]{:S(2)}) async-start(), calls=%async_computation.4 | async-start | bytes 1081344 | tf_op jit(solution)/shard_map/all_gather | solution.py:31
  40.0 369.3 %all-gather.4.cloned.1.call-start = ((), (), s32[]{:S(2)}) async-start(), calls=%async_computation.2 | async-start | bytes 1081344 | tf_op jit(solution)/shard_map/all_gather | solution.py:31
  40.8 588.9 %reduce-scatter.5.cloned.1.call-start = ((), (), s32[]{:S(2)}) async-start(), calls=%async_computation.5 | async-start | bytes 2162688 | tf_op jit(solution)/shard_map/reduce_scatter | solution.py:41
  349.4 0.7 copy-start.1
  351.6 3.9 copy-start.6
  630.6 83.8 %copy-start.2 = (bf16[32,32,128]{2,1,0:T(8,128)(2,1)S(1)}, bf16[32,32,128]{2,1,0:T(8,128)(2,1)}, u32[]{:S(2)}) copy-start(bf16[32,32,128]{2,1,0:T(8,128)(2,1)} %copy-done.1) | copy-start | bytes 786436
  630.6 83.9 %copy-start.3 = (f32[4,32,128]{2,1,0:T(8,128)S(1)}, f32[4,32,128]{2,1,0:T(8,128)}, u32[]{:S(2)}) copy-start(f32[4,32,128]{2,1,0:T(8,128)} %reduce-scatter.5.cloned.1.call-done) | copy-start | bytes 196612
Sparse Core Ops, SparseCore 0:
  39.4 215.2 reduce-scatter.2
  257.3 74.8 all-gather.5
  335.4 73.8 all-gather.3
  413.5 216.0 reduce-scatter.4
